TPU v7x, 128 devices: a whole 4x4x4 slice. The times are simulated.
128 devices in a mesh: dp: 32 (over y_lo, z, x), mp: 4 (over y_hi, core).
Axes of the slice: x: 4, y: 4 (y_hi: 2, y_lo: 2; y = y_hi * 2 + y_lo), z: 4, core: 2. Of those that a mesh axis runs over, the one named last changes fastest.
Arguments:
- layer_inputs: bfloat16 [16384, 8192], P('dp', 'mp'), may hold values from -54 to 54
- out_grads: bfloat16 [16384, 28672], P('dp', 'mp'), may hold values from -54 to 54
- loss_mask: int32 [16384], P('dp'), may hold values 0 or 1
- start_in: int32 [64, 8192], P(None, 'mp'), may hold values from -127 to 127
- start_out: int32 [64, 28672], P(None, 'mp'), may hold values from -127 to 127
Outputs:
- features: float32 [64, 4096], P('dp', 'mp')
- basis_in: float32 [64, 8192], P(None, 'mp')
- basis_out: float32 [64, 28672], P(None, 'mp')
All inputs are finite; a program needn't handle non-finite values. No bound on the sum of `loss_mask` on one device may be relied on, other than what follows from the above.
Results may differ from a plain program's by a relative error of at most 0.0065.
Values may be sent and summed in bfloat16 or wider, within the bound.
No kernel may reach another device: no remote copies, remote signals or barrier semaphores. Data moves between devices by JAX's collectives and lax.ppermute only.
A program may use at most 64 MiB of HBM per device.

v0:
```python
import jax
import jax.numpy as jnp
from jax import lax
from jax.sharding import PartitionSpec as P

ITERS = 2
LEN = 256


def coords_of(data, basis_half):
    return lax.dot_general(
        data, basis_half, (((1,), (1,)), ((), ())), preferred_element_type=jnp.float32
    )


def image_of(coords_half, data):
    return lax.dot_general(
        coords_half, data, (((0,), (0,)), ((), ())), preferred_element_type=jnp.float32
    )


def gram_of(image):
    return jnp.dot(image, image.T, precision=lax.Precision.HIGHEST)


def normalize(gram, image):
    lower = jnp.linalg.cholesky(gram)
    return jax.scipy.linalg.solve_triangular(lower, image, lower=True)


def shards(layer_inputs, out_grads, loss_mask, start_in, start_out):
    keep = loss_mask.astype(jnp.float32)[:, None]
    basis_in = start_in.astype(jnp.float32) / 128.0
    basis_out = start_out.astype(jnp.float32) / 128.0
    half_in = basis_in.astype(jnp.bfloat16)
    half_out = basis_out.astype(jnp.bfloat16)
    for step in range(ITERS):
        in_coords = coords_of(layer_inputs, half_in)
        out_coords = coords_of(out_grads, half_out) * keep
        in_coords, out_coords = lax.psum((in_coords, out_coords), "mp")
        in_image = image_of(in_coords.astype(jnp.bfloat16), layer_inputs)
        out_image = image_of(out_coords.astype(jnp.bfloat16), out_grads)
        out_owned = lax.psum_scatter(out_image, "dp", scatter_dimension=1, tiled=True)
        in_whole = lax.psum(in_image, "dp")
        gram_in = lax.psum(gram_of(in_whole), "mp")
        gram_out = lax.psum(gram_of(out_owned), ("dp", "mp"))
        new_in = normalize(gram_in, in_whole)
        new_out = normalize(gram_out, out_owned)
        if step + 1 < ITERS:
            half_in = new_in.astype(jnp.bfloat16)
            half_out = lax.all_gather(new_out.astype(jnp.bfloat16), "dp", axis=1, tiled=True)
        else:
            basis_in = new_in
            basis_out = lax.all_gather(new_out, "dp", axis=1, tiled=True)
    half_in = basis_in.astype(jnp.bfloat16)
    half_out = basis_out.astype(jnp.bfloat16)
    proj_in = coords_of(layer_inputs, half_in)
    proj_out = coords_of(out_grads, half_out) * keep
    rank = half_in.shape[0]
    seq_count = layer_inputs.shape[0] // LEN
    proj_in, proj_out = lax.psum((proj_in, proj_out), "mp")
    block = rank // lax.axis_size("mp")
    first = lax.axis_index("mp") * block
    part_in = lax.dynamic_slice_in_dim(proj_in.astype(jnp.bfloat16), first, block, 1)
    seq_in = part_in.reshape(seq_count, LEN, block)
    seq_out = proj_out.astype(jnp.bfloat16).reshape(seq_count, LEN, rank)
    summed = jnp.einsum("sti,stj->sij", seq_in, seq_out, preferred_element_type=jnp.float32) / LEN
    features = summed.reshape(seq_count, block * rank)
    return (features, basis_in, basis_out)


def solution(mesh):
    in_specs = (P("dp", "mp"), P("dp", "mp"), P("dp"), P(None, "mp"), P(None, "mp"))
    out_specs = (P("dp", "mp"), P(None, "mp"), P(None, "mp"))
    return jax.shard_map(shards, mesh=mesh, in_specs=in_specs, out_specs=out_specs, check_vma=False)
```

profile of v0, /device:TPU:1, one launch (start us, length us, event | category | flops | bytes accessed | tf_op | source)
XLA Modules:
  0.0 1492.7 jit_solution(5499521624738872316)
XLA Ops:
  8.8 1.8 convolution_bitcast_fusion.4
  10.6 15.8 %all-reduce.13 = bf16[512,64]{0,1:T(8,128)(2,1)S(1)} all-reduce(f32[512,64]{0,1:T(8,128)S(1)} %convolution_bitcast_fusion.4), channel_id=1, replica_groups=mesh['dp'=32,'mp'=4] {'mp'}, use_global_device_ids=true, to_apply=%region_0.0 | all-reduce | flops 32768 | bytes 196608 | tf_op jit(solution)/shard_map/psum | solution.py:40
  27.7 6.0 fusion.2
  33.7 285.4 %all-reduce.10.cloned.1.call-done = f32[64,2048]{1,0:T(8,128)} async-done(((f32[64,2048]{1,0:T(8,128)}), f32[64,2048]{1,0:T(8,128)}) %all-reduce.10.cloned.1.call-update) | async-done | bytes 524304 | tf_op jit(solution)/shard_map/psum | solution.py:44
  320.9 34.3 %psum.86 = f32[64,64]{0,1:T(8,128)S(1)} all-reduce(f32[64,64]{0,1:T(8,128)S(1)} %fusion.41), channel_id=1, replica_groups=mesh['dp'=32,'mp'=4] {'mp'}, use_global_device_ids=true, to_apply=%region_2.0 | all-reduce | flops 4096 | bytes 32768 | tf_op jit(solution)/shard_map/psum | solution.py:45
  355.3 5.8 cholesky.74
  362.5 4.9 custom-call.10
  369.8 16.8 %all-reduce.14 = (bf16[512,64]{0,1:T(8,128)(2,1)S(1)}, bf16[512,64]{0,1:T(8,128)(2,1)S(1)}) all-reduce(f32[512,64]{0,1:T(8,128)S(1)} %fusion.2, f32[512,64]{0,1:T(8,128)S(1)} %convolution_bitcast_fusion.3), channel_id=1, replica_groups=mesh['dp'=32,'mp'=4] {'mp'}, use_global_device_ids=true, to_apply=%region_9.12 | all-reduce | flops 65536 | bytes 393216 | tf_op jit(solution)/shard_map/psum | solution.py:40
  388.0 7.9 convolution_bitcast_fusion.1
  395.9 281.3 %all-reduce.12.cloned.1.call-done = f32[64,2048]{1,0:T(8,128)} async-done(((f32[64,2048]{1,0:T(8,128)}), f32[64,2048]{1,0:T(8,128)}) %all-reduce.12.cloned.1.call-update) | async-done | bytes 524304 | tf_op jit(solution)/shard_map/psum | solution.py:44
  677.2 1.8 fusion.42
  679.0 167.0 %reduce-scatter.7.cloned.1.call-done = f32[224,64]{1,0:T(8,128)} async-done(((f32[7168,64]{1,0:T(8,128)}), f32[224,64]{1,0:T(8,128)}) %reduce-scatter.7.cloned.1.call-update) | async-done | bytes 57360
  847.4 86.2 %psum.92 = f32[64,64]{0,1:T(8,128)S(1)} all-reduce(f32[64,64]{0,1:T(8,128)S(1)} %fusion.11), channel_id=1, replica_groups=mesh['dp'=32,'mp'=4] {'dp','mp'}, use_global_device_ids=true, to_apply=%region_11.14 | all-reduce | flops 4096 | bytes 32768 | tf_op jit(solution)/shard_map/psum | solution.py:46
  933.6 5.8 cholesky.96
  940.8 4.9 custom-call.12
  947.0 69.9 %all-gather = bf16[32,224,64]{1,2,0:T(8,128)(2,1)S(1)} all-gather(bf16[1,224,64]{1,2,0:T(8,128)(2,1)S(1)} %fusion.3), channel_id=1, replica_groups=mesh['dp'=32,'mp'=4] {'dp'}, dimensions={0}, use_global_device_ids=true | all-gather | bytes 946176 | tf_op jit(solution)/shard_map/all_gather | solution.py:51
  1017.5 2.8 reshape.31
  1020.2 5.7 fusion.1
  1026.0 28.4 %all-reduce.15 = (bf16[512,64]{0,1:T(8,128)(2,1)S(1)}, f32[64,64]{0,1:T(8,128)S(1)}) all-reduce(f32[512,64]{0,1:T(8,128)S(1)} %fusion.1, f32[64,64]{0,1:T(8,128)S(1)} %fusion.42), channel_id=1, replica_groups=mesh['dp'=32,'mp'=4] {'mp'}, use_global_device_ids=true, to_apply=%region_12.0 | all-reduce | flops 36864 | bytes 229376 | tf_op jit(solution)/shard_map/psum | solution.py:40
  1054.4 7.9 convolution_bitcast_fusion
  1062.4 140.7 %reduce-scatter.9.cloned.1.call-done = f32[224,64]{1,0:T(8,128)} async-done(((f32[7168,64]{1,0:T(8,128)}), f32[224,64]{1,0:T(8,128)}) %reduce-scatter.9.cloned.1.call-update) | async-done | bytes 57360
  1204.4 86.6 %psum.94 = f32[64,64]{0,1:T(8,128)S(1)} all-reduce(f32[64,64]{0,1:T(8,128)S(1)} %fusion.8), channel_id=1, replica_groups=mesh['dp'=32,'mp'=4] {'dp','mp'}, use_global_device_ids=true, to_apply=%region_14.18 | all-reduce | flops 4096 | bytes 32768 | tf_op jit(solution)/shard_map/psum | solution.py:46
  1291.1 5.8 cholesky.107
  1298.3 4.9 custom-call.13
  1303.2 1.9 convolution_bitcast_fusion.5
  1305.2 5.8 cholesky.85
  1312.4 4.9 custom-call.11
  1318.7 114.7 %all-gather.4.cloned.1.call-done = f32[32,224,64]{1,2,0:T(8,128)} async-done(((f32[1,224,64]{1,2,0:T(8,128)}), f32[32,224,64]{1,2,0:T(8,128)}) %all-gather.4.cloned.1.call-update) | async-done | bytes 1835024 | tf_op jit(solution)/shard_map/all_gather | solution.py:54
  1433.4 4.1 copy.38
  1437.5 3.5 reshape.33
  1441.0 6.0 fusion
  1446.9 38.4 %all-reduce.16 = (bf16[512,64]{0,1:T(8,128)(2,1)S(1)}, bf16[512,64]{0,1:T(8,128)(2,1)S(1)}) all-reduce(f32[512,64]{0,1:T(8,128)S(1)} %fusion, f32[512,64]{0,1:T(8,128)S(1)} %convolution_bitcast_fusion.2), channel_id=1, replica_groups=mesh['dp'=32,'mp'=4] {'mp'}, use_global_device_ids=true, to_apply=%region_15.19 | all-reduce | flops 65536 | bytes 393216 | tf_op jit(solution)/shard_map/psum | solution.py:61
  (53 shorter events, 21.0 us)
Async XLA Ops:
  7.2 1.6 copy-start
  7.2 312.0 %all-reduce.10.cloned.1.call-start = ((), (), s32[]{:S(2)}) async-start(), calls=%async_computation.2 | async-start | bytes 1048576 | tf_op jit(solution)/shard_map/psum | solution.py:44
  10.6 17.1 %copy-start.3 = (s32[512]{0:T(512)S(1)}, s32[512]{0:T(512)}, u32[]{:S(2)}) copy-start(s32[512]{0:T(512)} %param.12) | copy-start | bytes 6148
  27.6 649.6 %all-reduce.12.cloned.1.call-start = ((), (), s32[]{:S(2)}) async-start(), calls=%async_computation.3 | async-start | bytes 1048576 | tf_op jit(solution)/shard_map/psum | solution.py:44
  387.9 458.1 %reduce-scatter.7.cloned.1.call-start = ((), (), s32[]{:S(2)}) async-start(), calls=%async_computation.5 | async-start | bytes 3784704
  395.9 807.2 %reduce-scatter.9.cloned.1.call-start = ((), (), s32[]{:S(2)}) async-start(), calls=%async_computation.6 | async-start | bytes 3784704
  1062.3 255.0 %copy-start.1 = (f32[64,2048]{1,0:T(8,128)S(1)}, f32[64,2048]{1,0:T(8,128)}, u32[]{:S(2)}) copy-start(f32[64,2048]{1,0:T(8,128)} %all-reduce.12.cloned.1.call-done) | copy-start | bytes 1572868
  1062.3 371.1 %all-gather.4.cloned.1.call-start = ((), (), s32[]{:S(2)}) async-start(), calls=%async_computation.4 | async-start | bytes 2162688 | tf_op jit(solution)/shard_map/all_gather | solution.py:54
  1318.0 119.6 %copy-start.2 = (f32[64,2048]{1,0:T(8,128)}, f32[64,2048]{1,0:T(8,128)S(1)}, u32[]{:S(2)}) copy-start(f32[64,2048]{1,0:T(8,128)S(1)} %fusion.30) | copy-start | bytes 1572868
Sparse Core Ops, SparseCore 0:
  27.8 291.3 all-reduce.9
  388.0 289.1 all-reduce.11
  679.6 166.3 reduce-scatter.6
  1062.4 140.6 reduce-scatter.8
  1305.2 128.1 all-gather.3
where the time goes:
time: 1490 us
  waiting for transfers between devices  989 us (66%)
  blocking collectives  376 us (25%)
  matrix products  51.1 us (3%)
  other arithmetic  48.3 us (3%)
    psum x2, waiting for transfers between devices, shards(): in_whole = lax.psum(in_image, 'dp')  567 us
    unnamed x7, waiting for transfers between devices  308 us
    psum x2, blocking collectives, shards(): gram_out = lax.psum(gram_of(out_owned), ('dp', 'mp'))  173 us
    all_gather x1, waiting for transfers between devices, shards(): basis_out = lax.all_gather(new_out, 'dp', axis=1, tiled=True)  115 us
    all_gather x1, blocking collectives, shards(): lax.all_gather(new_out.astype(jnp.bfloat16), 'dp', axis=1, tiled=True)  69.9 us
    psum x3, blocking collectives, shards(): in_coords, out_coords = lax.psum((in_coords, out_coords), 'mp')  61 us
    psum x1, blocking collectives, shards(): proj_in, proj_out = lax.psum((proj_in, proj_out), 'mp')  38.4 us
    psum x1, blocking collectives, shards(): gram_in = lax.psum(gram_of(in_whole), 'mp')  34.3 us
  transfers between devices with their start and end apart: 5, of which 5 were waited for; matrix products, arithmetic and copies ran while one was open for 2% of the time, Pallas kernels for 0%

commit v1 on v0

--- a/solution.py
+++ b/solution.py
@@ -51,7 +51,10 @@
             half_out = lax.all_gather(new_out.astype(jnp.bfloat16), "dp", axis=1, tiled=True)
         else:
             basis_in = new_in
-            basis_out = lax.all_gather(new_out, "dp", axis=1, tiled=True)
+            peers = lax.axis_size("dp")
+            blocks = jnp.stack([new_out for _ in range(peers)])
+            blocks = lax.all_to_all(blocks, "dp", split_axis=0, concat_axis=0)
+            basis_out = jnp.concatenate(blocks, axis=1)
     half_in = basis_in.astype(jnp.bfloat16)
     half_out = basis_out.astype(jnp.bfloat16)
     proj_in = coords_of(layer_inputs, half_in)

time: 1490 us -> 1380 us (0.926)
  waiting for transfers between devices: 989 us -> 887 us
  blocking collectives: 376 us -> 356 us
    all_gather x1 -> x0, waiting for transfers between devices: 115 us -> none  [shards(): basis_out = lax.all_gather(new_out, 'dp', axis=1, tiled=True)]
    psum x1, blocking collectives: 38.4 us -> 17.9 us  [shards(): proj_in, proj_out = lax.psum((proj_in, proj_out), 'mp')]
    unnamed x7 -> x6, waiting for transfers between devices: 308 us -> 307 us
where the time goes in v1:
time: 1380 us
  waiting for transfers between devices  887 us (64%)
  blocking collectives  356 us (26%)
  matrix products  50.5 us (4%)
  other arithmetic  48.3 us (4%)
  local copies, waits for them, and re-layouts  15 us (1%)
  between operations  14 us (1%)
    psum x2, waiting for transfers between devices, shards(): in_whole = lax.psum(in_image, 'dp')  567 us
    unnamed x6, waiting for transfers between devices  307 us
    psum x2, blocking collectives, shards(): gram_out = lax.psum(gram_of(out_owned), ('dp', 'mp'))  173 us
    all_gather x1, blocking collectives, shards(): lax.all_gather(new_out.astype(jnp.bfloat16), 'dp', axis=1, tiled=True)  69.9 us
    psum x3, blocking collectives, shards(): in_coords, out_coords = lax.psum((in_coords, out_coords), 'mp')  61 us
    psum x1, blocking collectives, shards(): gram_in = lax.psum(gram_of(in_whole), 'mp')  34.3 us
  transfers between devices with their start and end apart: 5, of which 5 were waited for; matrix products, arithmetic and copies ran while one was open for 2% of the time, Pallas kernels for 0%

profile of v1, /device:TPU:1, one launch (start us, length us, event | category | flops | bytes accessed | tf_op | source)
XLA Modules:
  0.0 1376.6 jit_solution(13789868344534174123)
XLA Ops:
  8.8 1.8 convolution_bitcast_fusion.4
  10.6 15.8 %all-reduce.13 = bf16[512,64]{0,1:T(8,128)(2,1)S(1)} all-reduce(f32[512,64]{0,1:T(8,128)S(1)} %convolution_bitcast_fusion.4), channel_id=1, replica_groups=mesh['dp'=32,'mp'=4] {'mp'}, use_global_device_ids=true, to_apply=%region_0.0 | all-reduce | flops 32768 | bytes 196608 | tf_op jit(solution)/shard_map/psum | solution.py:40
  27.7 6.0 fusion.2
  33.7 285.4 %all-reduce.10.cloned.1.call-done = f32[64,2048]{1,0:T(8,128)} async-done(((f32[64,2048]{1,0:T(8,128)}), f32[64,2048]{1,0:T(8,128)}) %all-reduce.10.cloned.1.call-update) | async-done | bytes 524304 | tf_op jit(solution)/shard_map/psum | solution.py:44
  320.9 34.3 %psum.86 = f32[64,64]{0,1:T(8,128)S(1)} all-reduce(f32[64,64]{0,1:T(8,128)S(1)} %fusion.42), channel_id=1, replica_groups=mesh['dp'=32,'mp'=4] {'mp'}, use_global_device_ids=true, to_apply=%region_2.0 | all-reduce | flops 4096 | bytes 32768 | tf_op jit(solution)/shard_map/psum | solution.py:45
  355.3 5.8 cholesky.74
  362.5 4.9 custom-call.10
  369.8 16.8 %all-reduce.14 = (bf16[512,64]{0,1:T(8,128)(2,1)S(1)}, bf16[512,64]{0,1:T(8,128)(2,1)S(1)}) all-reduce(f32[512,64]{0,1:T(8,128)S(1)} %fusion.2, f32[512,64]{0,1:T(8,128)S(1)} %convolution_bitcast_fusion.3), channel_id=1, replica_groups=mesh['dp'=32,'mp'=4] {'mp'}, use_global_device_ids=true, to_apply=%region_9.12 | all-reduce | flops 65536 | bytes 393216 | tf_op jit(solution)/shard_map/psum | solution.py:40
  388.0 7.9 convolution_bitcast_fusion.1
  395.9 281.3 %all-reduce.12.cloned.1.call-done = f32[64,2048]{1,0:T(8,128)} async-done(((f32[64,2048]{1,0:T(8,128)}), f32[64,2048]{1,0:T(8,128)}) %all-reduce.12.cloned.1.call-update) | async-done | bytes 524304 | tf_op jit(solution)/shard_map/psum | solution.py:44
  677.2 1.8 fusion.43
  679.0 167.0 %reduce-scatter.7.cloned.1.call-done = f32[224,64]{1,0:T(8,128)} async-done(((f32[7168,64]{1,0:T(8,128)}), f32[224,64]{1,0:T(8,128)}) %reduce-scatter.7.cloned.1.call-update) | async-done | bytes 57360
  847.4 86.2 %psum.92 = f32[64,64]{0,1:T(8,128)S(1)} all-reduce(f32[64,64]{0,1:T(8,128)S(1)} %fusion.12), channel_id=1, replica_groups=mesh['dp'=32,'mp'=4] {'dp','mp'}, use_global_device_ids=true, to_apply=%region_11.14 | all-reduce | flops 4096 | bytes 32768 | tf_op jit(solution)/shard_map/psum | solution.py:46
  933.6 5.8 cholesky.96
  940.8 4.9 custom-call.12
  947.0 69.9 %all-gather = bf16[32,224,64]{1,2,0:T(8,128)(2,1)S(1)} all-gather(bf16[1,224,64]{1,2,0:T(8,128)(2,1)S(1)} %fusion.3), channel_id=1, replica_groups=mesh['dp'=32,'mp'=4] {'dp'}, dimensions={0}, use_global_device_ids=true | all-gather | bytes 946176 | tf_op jit(solution)/shard_map/all_gather | solution.py:51
  1017.5 2.8 reshape.41
  1020.2 5.7 fusion.1
  1026.0 28.4 %all-reduce.15 = (bf16[512,64]{0,1:T(8,128)(2,1)S(1)}, f32[64,64]{0,1:T(8,128)S(1)}) all-reduce(f32[512,64]{0,1:T(8,128)S(1)} %fusion.1, f32[64,64]{0,1:T(8,128)S(1)} %fusion.43), channel_id=1, replica_groups=mesh['dp'=32,'mp'=4] {'mp'}, use_global_device_ids=true, to_apply=%region_12.0 | all-reduce | flops 36864 | bytes 229376 | tf_op jit(solution)/shard_map/psum | solution.py:40
  1054.4 7.9 convolution_bitcast_fusion
  1062.3 140.0 %reduce-scatter.9.cloned.1.call-done = f32[224,64]{1,0:T(8,128)} async-done(((f32[7168,64]{1,0:T(8,128)}), f32[224,64]{1,0:T(8,128)}) %reduce-scatter.9.cloned.1.call-update) | async-done | bytes 57360
  1203.7 87.1 %psum.94 = f32[64,64]{0,1:T(8,128)S(1)} all-reduce(f32[64,64]{0,1:T(8,128)S(1)} %fusion.8), channel_id=1, replica_groups=mesh['dp'=32,'mp'=4] {'dp','mp'}, use_global_device_ids=true, to_apply=%region_14.18 | all-reduce | flops 4096 | bytes 32768 | tf_op jit(solution)/shard_map/psum | solution.py:46
  1290.9 5.8 cholesky.107
  1298.1 4.9 custom-call.13
  1305.8 4.9 all-to-all-start
  1310.8 5.8 cholesky.85
  1318.0 4.9 custom-call.11
  1324.3 13.5 all-to-all-done
  1337.8 4.1 copy.48
  1341.9 3.5 reshape.37
  1345.3 6.0 fusion
  1351.3 17.9 %all-reduce.16 = (bf16[512,64]{0,1:T(8,128)(2,1)S(1)}, bf16[512,64]{0,1:T(8,128)(2,1)S(1)}) all-reduce(f32[512,64]{0,1:T(8,128)S(1)} %fusion, f32[512,64]{0,1:T(8,128)S(1)} %convolution_bitcast_fusion.2), channel_id=1, replica_groups=mesh['dp'=32,'mp'=4] {'mp'}, use_global_device_ids=true, to_apply=%region_15.19 | all-reduce | flops 65536 | bytes 393216 | tf_op jit(solution)/shard_map/psum | solution.py:64
  (53 shorter events, 23.7 us)
Async XLA Ops:
  7.2 1.6 copy-start
  7.2 312.0 %all-reduce.10.cloned.1.call-start = ((), (), s32[]{:S(2)}) async-start(), calls=%async_computation.3 | async-start | bytes 1048576 | tf_op jit(solution)/shard_map/psum | solution.py:44
  10.6 17.1 %copy-start.3 = (s32[512]{0:T(512)S(1)}, s32[512]{0:T(512)}, u32[]{:S(2)}) copy-start(s32[512]{0:T(512)} %param.12) | copy-start | bytes 6148
  27.6 649.6 %all-reduce.12.cloned.1.call-start = ((), (), s32[]{:S(2)}) async-start(), calls=%async_computation.4 | async-start | bytes 1048576 | tf_op jit(solution)/shard_map/psum | solution.py:44
  387.9 458.1 %reduce-scatter.7.cloned.1.call-start = ((), (), s32[]{:S(2)}) async-start(), calls=%async_computation.5 | async-start | bytes 3784704
  395.9 806.5 %reduce-scatter.9.cloned.1.call-start = ((), (), s32[]{:S(2)}) async-start(), calls=%async_computation.6 | async-start | bytes 3784704
  1305.8 17.1 %copy-start.1 = (f32[64,2048]{1,0:T(8,128)S(1)}, f32[64,2048]{1,0:T(8,128)}, u32[]{:S(2)}) copy-start(f32[64,2048]{1,0:T(8,128)} %all-reduce.12.cloned.1.call-done) | copy-start | bytes 1572868
  1305.8 32.0 %all-to-all-start = ((f32[32,64,224]{2,1,0:T(8,128)}), f32[32,64,224]{2,1,0:T(8,128)}, u32[]{:S(2)}, u32[]{:S(2)}) async-start(f32[32,64,224]{2,1,0:T(8,128)} %stack.2), calls=%async_computation | async-start | bytes 4194304 | tf_op jit(solution)/shard_map/all_to_all | solution.py:56
  1323.5 18.3 %copy-start.2 = (f32[64,2048]{1,0:T(8,128)}, f32[64,2048]{1,0:T(8,128)S(1)}, u32[]{:S(2)}) copy-start(f32[64,2048]{1,0:T(8,128)S(1)} %fusion.31) | copy-start | bytes 1572868
Sparse Core Ops, SparseCore 0:
  27.8 291.3 all-reduce.9
  388.0 289.1 all-reduce.11
  679.6 166.3 reduce-scatter.6
  1062.4 139.8 reduce-scatter.8
